TPU v7x, 128 devices: a whole 4x4x4 slice. The times are simulated.
128 devices in a mesh: row: 16 (over z_lo, y, core), col: 8 (over x, z_hi).
Axes of the slice: x: 4, y: 4, z: 4 (z_hi: 2, z_lo: 2; z = z_hi * 2 + z_lo), core: 2. Of those that a mesh axis runs over, the one named last changes fastest.
Arguments:
- features: bfloat16 [32768, 128], P(('col', 'row')), may hold values from -6 to 6
- weight: bfloat16 [128, 256], replicated, may hold values from -0.5 to 0.5
- adj_values: bfloat16 [12288, 256, 256], P(('row', 'col')), may hold values from -0.0390625 to 0.0390625
- slot_rows: int32 [12288], P(('row', 'col')), may hold values from 0 to 7, as said below
- slot_cols: int32 [12288], P(('row', 'col')), may hold values from 0 to 15
- slot_live: int32 [128], P(('row', 'col')), may hold values from 13 to 96, as said below
- cotangent: bfloat16 [32768, 256], P(('row', 'col')), may hold values from -6 to 6
Outputs:
- output: bfloat16 [32768, 256], P(('row', 'col'))
- grad_features: bfloat16 [32768, 128], P(('col', 'row'))
- grad_weight: float32 [128, 256], replicated
Inputs may be any that keep to these rules, and one draw needn't show every extreme that they name: Within one device's slots the pairs (slot_rows, slot_cols) are distinct. `slot_live`: some device has all 96 slots live.
All inputs are finite; a program needn't handle non-finite values.
Results may differ from a plain program's by a relative error of at most 0.006.
Values may be sent and summed in bfloat16 or wider, within the bound.
A program may use at most 128 MiB of HBM per device.

v0:
```python
import math
import jax
import jax.numpy as jnp
from jax import lax
from jax.sharding import PartitionSpec as P


def silu_slope(value):
    sig = jax.nn.sigmoid(value)
    return sig * (1.0 + value * (1.0 - sig))


def block_product(adj_values, index_in, index_out, keep, source, count_out, transposed):
    slots, size = (adj_values.shape[0], adj_values.shape[1])
    width = source.shape[2]
    group = math.gcd(slots, 32)
    groups = slots // group

    def step(total, item):
        values, taken, placed, weights = item
        picked = source[taken]
        if transposed:
            product = jnp.einsum("sab,saf->sbf", values, picked, preferred_element_type=jnp.float32)
        else:
            product = jnp.einsum("sab,sbf->saf", values, picked, preferred_element_type=jnp.float32)
        return (total.at[placed].add(product * weights[:, None, None]), None)

    items = (
        adj_values.reshape(groups, group, size, size),
        index_in.reshape(groups, group),
        index_out.reshape(groups, group),
        keep.reshape(groups, group),
    )
    total, _ = lax.scan(step, jnp.zeros((count_out, size, width), jnp.float32), items)
    return total.reshape(count_out * size, width)


def body(features, weight, adj_values, slot_rows, slot_cols, slot_live, cotangent):
    size = adj_values.shape[1]
    slots = adj_values.shape[0]
    width = weight.shape[1]
    own_rows = features.shape[0]
    per_device = own_rows // size
    tile_rows = per_device * lax.axis_size("col")
    tile_cols = per_device * lax.axis_size("row")
    nodes = own_rows * lax.axis_size("row") * lax.axis_size("col")
    keep = (jnp.arange(slots, dtype=jnp.int32) < slot_live[0]).astype(jnp.float32)
    projected = jnp.dot(features, weight, preferred_element_type=jnp.float32).astype(jnp.bfloat16)
    column_rows = lax.all_gather(projected, "row", axis=0, tiled=True)
    column_blocks = column_rows.reshape(tile_cols, size, width)
    partial_value = block_product(
        adj_values, slot_cols, slot_rows, keep, column_blocks, tile_rows, False
    )
    summed = lax.psum_scatter(partial_value, "col", scatter_dimension=0, tiled=True)
    output = jax.nn.silu(summed).astype(jnp.bfloat16)
    grad_summed = (cotangent.astype(jnp.float32) * silu_slope(summed)).astype(jnp.bfloat16)
    grad_range = lax.all_gather(grad_summed, "col", axis=0, tiled=True)
    grad_blocks = grad_range.reshape(tile_rows, size, width)
    back = block_product(adj_values, slot_rows, slot_cols, keep, grad_blocks, tile_cols, True)
    grad_projected = lax.psum_scatter(back, "row", scatter_dimension=0, tiled=True).astype(
        jnp.bfloat16
    )
    grad_features = jnp.dot(grad_projected, weight.T, preferred_element_type=jnp.float32).astype(
        jnp.bfloat16
    )
    local_term = lax.dot_general(
        features, grad_projected, (((0,), (0,)), ((), ())), preferred_element_type=jnp.float32
    )
    grad_weight = lax.psum(local_term, ("row", "col")) / math.sqrt(nodes)
    return (output, grad_features, grad_weight)


def solution(mesh):
    placed = (
        P(("col", "row"), None),
        P(),
        P(("row", "col"), None, None),
        P(("row", "col")),
        P(("row", "col")),
        P(("row", "col")),
        P(("row", "col"), None),
    )
    return jax.shard_map(
        body,
        mesh=mesh,
        in_specs=placed,
        out_specs=(P(("row", "col"), None), P(("col", "row"), None), P()),
        check_vma=False,
    )
```

profile of v0, /device:TPU:1, one launch (start us, length us, event | category | flops | bytes accessed | tf_op | source)
XLA Modules:
  0.0 557.0 jit_solution(4911130216952027264)
XLA Ops:
  7.2 0.0 all-gather.3.cloned.1.call-start
  7.2 0.8 copy-done
  8.0 1.7 convolution_convert_fusion
  9.7 0.0 all-gather.3.cloned.1.call-update
  9.7 0.0 reduce-scatter.3.cloned.1.call-start
  10.4 0.7 reshape.149
  11.1 0.7 reshape.151
  11.9 35.7 %all-gather.3.cloned.1.call-done = bf16[4096,256]{1,0:T(8,128)(2,1)} async-done(((bf16[256,256]{1,0:T(8,128)(2,1)}), bf16[4096,256]{1,0:T(8,128)(2,1)}) %all-gather.3.cloned.1.call-update) | async-done | bytes 2097168 | tf_op jit(solution)/shard_map/all_gather | solution.py:49
  47.6 0.2 broadcast_in_dim.4
  47.8 72.4 %while.20 = (s32[]{:T(128)}, f32[8,256,256]{2,1,0:T(8,128)S(1)}, s32[3,32]{1,0:T(4,128)S(1)}, bf16[3,32,256,256]{3,2,1,0:T(8,128)(2,1)}, s32[3,32]{1,0:T(4,128)S...) while((s32[]{:T(128)}, f32[8,256,256]{2,1,0:T(8,128)S(1)}, s32[3,32]{1,0:T(4,128)S(1)}, ...), condition=%wide.region_2.3_spmd, body=%wide.region_0.2_spmd.sunk | while | flops 1077937408 | bytes 50337628 | solution.py:34
  47.8 4.4 gather_fusion
  52.2 7.9 %broadcast_multiply_fusion.5 = f32[32,256,256]{2,1,0:T(8,128)} fusion(f32[32]{0:T(128)S(1)} %fusion.42, bf16[32,256,256]{2,1,0:T(8,128)(2,1)} %gather_fusion, bf16[3,32,256,256]{3,2,1,0:T(8,128)(2,1)} %get-tuple-element.236, s32[]{:T(128)} %get-tuple-element.225), kind=kOutput, calls=%fused_computation.6.clone.1 | convolution fusion | flops 1075838976 | bytes 16777856 | tf_op jit(solution)/shard_map/while/body/eval_jaxpr/sab,sbf->saf/dot_general | solution.py:25
  60.2 11.8 %scatter_fusion = f32[8,256,256]{2,1,0:T(8,128)S(1)} fusion(f32[8,256,256]{2,1,0:T(8,128)S(1)} %get-tuple-element.226, s32[32]{0:T(128)S(1)} %get-tuple-element.206, f32[32,256,256]{2,1,0:T(8,128)} %broadcast_multiply_fusion.5), kind=kCustom, calls=%fused_computation.2.clone.1 | custom fusion | flops 2097152 | bytes 25165952 | tf_op jit(solution)/shard_map/while/body/eval_jaxpr/scatter-add | solution.py:26
  72.0 4.4 gather_fusion
  76.4 7.9 %broadcast_multiply_fusion.5 = f32[32,256,256]{2,1,0:T(8,128)} fusion(f32[32]{0:T(128)S(1)} %fusion.42, bf16[32,256,256]{2,1,0:T(8,128)(2,1)} %gather_fusion, bf16[3,32,256,256]{3,2,1,0:T(8,128)(2,1)} %get-tuple-element.236, s32[]{:T(128)} %get-tuple-element.225), kind=kOutput, calls=%fused_computation.6.clone.1 | convolution fusion | flops 1075838976 | bytes 16777856 | tf_op jit(solution)/shard_map/while/body/eval_jaxpr/sab,sbf->saf/dot_general | solution.py:25
  84.3 11.7 %scatter_fusion = f32[8,256,256]{2,1,0:T(8,128)S(1)} fusion(f32[8,256,256]{2,1,0:T(8,128)S(1)} %get-tuple-element.226, s32[32]{0:T(128)S(1)} %get-tuple-element.206, f32[32,256,256]{2,1,0:T(8,128)} %broadcast_multiply_fusion.5), kind=kCustom, calls=%fused_computation.2.clone.1 | custom fusion | flops 2097152 | bytes 25165952 | tf_op jit(solution)/shard_map/while/body/eval_jaxpr/scatter-add | solution.py:26
  96.1 4.4 gather_fusion
  100.5 7.9 %broadcast_multiply_fusion.5 = f32[32,256,256]{2,1,0:T(8,128)} fusion(f32[32]{0:T(128)S(1)} %fusion.42, bf16[32,256,256]{2,1,0:T(8,128)(2,1)} %gather_fusion, bf16[3,32,256,256]{3,2,1,0:T(8,128)(2,1)} %get-tuple-element.236, s32[]{:T(128)} %get-tuple-element.225), kind=kOutput, calls=%fused_computation.6.clone.1 | convolution fusion | flops 1075838976 | bytes 16777856 | tf_op jit(solution)/shard_map/while/body/eval_jaxpr/sab,sbf->saf/dot_general | solution.py:25
  108.4 11.7 %scatter_fusion = f32[8,256,256]{2,1,0:T(8,128)S(1)} fusion(f32[8,256,256]{2,1,0:T(8,128)S(1)} %get-tuple-element.226, s32[32]{0:T(128)S(1)} %get-tuple-element.206, f32[32,256,256]{2,1,0:T(8,128)} %broadcast_multiply_fusion.5), kind=kCustom, calls=%fused_computation.2.clone.1 | custom fusion | flops 2097152 | bytes 25165952 | tf_op jit(solution)/shard_map/while/body/eval_jaxpr/scatter-add | solution.py:26
  120.2 1.3 copy-done.1
  121.5 0.0 reduce-scatter.3.cloned.1.call-update
  121.6 0.0 all-gather.5.cloned.1.call-start
  121.6 75.0 %reduce-scatter.3.cloned.1.call-done = f32[256,256]{1,0:T(8,128)} async-done(((f32[2048,256]{1,0:T(8,128)}), f32[256,256]{1,0:T(8,128)}) %reduce-scatter.3.cloned.1.call-update) | async-done | bytes 262160 | tf_op jit(solution)/shard_map/reduce_scatter | solution.py:54
  196.6 1.8 multiply_convert_fusion
  198.4 0.0 all-gather.5.cloned.1.call-update
  198.4 0.0 reduce-scatter.5.cloned.1.call-start
  198.5 16.6 %copy.10 = bf16[96,256,256]{1,2,0:T(8,128)(2,1)} copy(bf16[96,256,256]{2,1,0:T(8,128)(2,1)} %bitcast.87) | data formatting | bytes 25165824 | tf_op args[2]
  215.1 30.2 %all-gather.5.cloned.1.call-done = bf16[2048,256]{1,0:T(8,128)(2,1)} async-done(((bf16[256,256]{1,0:T(8,128)(2,1)}), bf16[2048,256]{1,0:T(8,128)(2,1)}) %all-gather.5.cloned.1.call-update) | async-done | bytes 1048592 | tf_op jit(solution)/shard_map/all_gather | solution.py:57
  245.3 2.4 broadcast_in_dim.8
  247.7 87.2 %while.21 = (s32[]{:T(128)}, f32[16,256,256]{2,1,0:T(8,128)}, s32[3,32]{1,0:T(4,128)S(1)}, bf16[3,32,256,256]{2,3,1,0:T(8,128)(2,1)}, s32[3,32]{1,0:T(4,128)S(1)...) while((s32[]{:T(128)}, f32[16,256,256]{2,1,0:T(8,128)}, s32[3,32]{1,0:T(4,128)S(1)}, ...), condition=%wide.region_6.7_spmd, body=%wide.region_4.6_spmd.sunk | while | flops 1077937408 | bytes 50337628 | solution.py:34
  247.7 2.8 gather_fusion.1
  250.5 7.9 %broadcast_multiply_fusion.6 = f32[32,256,256]{2,1,0:T(8,128)} fusion(f32[32]{0:T(128)S(1)} %fusion.46, bf16[32,256,256]{2,1,0:T(8,128)(2,1)} %gather_fusion.1, bf16[3,32,256,256]{2,3,1,0:T(8,128)(2,1)} %get-tuple-element.260, s32[]{:T(128)} %get-tuple-element.249), kind=kOutput, calls=%fused_computation.22.clone.1 | convolution fusion | flops 1075838976 | bytes 16777856 | tf_op jit(solution)/shard_map/while/body/eval_jaxpr/sab,saf->sbf/dot_general | solution.py:23
  258.4 18.5 %scatter_fusion.1 = f32[16,256,256]{2,1,0:T(8,128)} fusion(f32[16,256,256]{2,1,0:T(8,128)} %get-tuple-element.250, s32[32]{0:T(128)S(1)} %get-tuple-element.215, f32[32,256,256]{2,1,0:T(8,128)} %broadcast_multiply_fusion.6), kind=kCustom, calls=%fused_computation.3.clone.1 | custom fusion | flops 2097152 | bytes 25165952 | tf_op jit(solution)/shard_map/while/body/eval_jaxpr/scatter-add | solution.py:26
  277.0 2.8 gather_fusion.1
  279.8 7.9 %broadcast_multiply_fusion.6 = f32[32,256,256]{2,1,0:T(8,128)} fusion(f32[32]{0:T(128)S(1)} %fusion.46, bf16[32,256,256]{2,1,0:T(8,128)(2,1)} %gather_fusion.1, bf16[3,32,256,256]{2,3,1,0:T(8,128)(2,1)} %get-tuple-element.260, s32[]{:T(128)} %get-tuple-element.249), kind=kOutput, calls=%fused_computation.22.clone.1 | convolution fusion | flops 1075838976 | bytes 16777856 | tf_op jit(solution)/shard_map/while/body/eval_jaxpr/sab,saf->sbf/dot_general | solution.py:23
  287.7 18.3 %scatter_fusion.1 = f32[16,256,256]{2,1,0:T(8,128)} fusion(f32[16,256,256]{2,1,0:T(8,128)} %get-tuple-element.250, s32[32]{0:T(128)S(1)} %get-tuple-element.215, f32[32,256,256]{2,1,0:T(8,128)} %broadcast_multiply_fusion.6), kind=kCustom, calls=%fused_computation.3.clone.1 | custom fusion | flops 2097152 | bytes 25165952 | tf_op jit(solution)/shard_map/while/body/eval_jaxpr/scatter-add | solution.py:26
  306.0 2.8 gather_fusion.1
  308.8 7.9 %broadcast_multiply_fusion.6 = f32[32,256,256]{2,1,0:T(8,128)} fusion(f32[32]{0:T(128)S(1)} %fusion.46, bf16[32,256,256]{2,1,0:T(8,128)(2,1)} %gather_fusion.1, bf16[3,32,256,256]{2,3,1,0:T(8,128)(2,1)} %get-tuple-element.260, s32[]{:T(128)} %get-tuple-element.249), kind=kOutput, calls=%fused_computation.22.clone.1 | convolution fusion | flops 1075838976 | bytes 16777856 | tf_op jit(solution)/shard_map/while/body/eval_jaxpr/sab,saf->sbf/dot_general | solution.py:23
  316.7 18.2 %scatter_fusion.1 = f32[16,256,256]{2,1,0:T(8,128)} fusion(f32[16,256,256]{2,1,0:T(8,128)} %get-tuple-element.250, s32[32]{0:T(128)S(1)} %get-tuple-element.215, f32[32,256,256]{2,1,0:T(8,128)} %broadcast_multiply_fusion.6), kind=kCustom, calls=%fused_computation.3.clone.1 | custom fusion | flops 2097152 | bytes 25165952 | tf_op jit(solution)/shard_map/while/body/eval_jaxpr/scatter-add | solution.py:26
  334.9 0.0 reduce-scatter.5.cloned.1.call-update
  335.0 0.0 all-reduce.2.cloned.1.call-start
  335.0 64.2 %reduce-scatter.5.cloned.1.call-done = f32[256,256]{1,0:T(8,128)} async-done(((f32[4096,256]{1,0:T(8,128)}), f32[256,256]{1,0:T(8,128)}) %reduce-scatter.5.cloned.1.call-update) | async-done | bytes 262160 | tf_op jit(solution)/shard_map/reduce_scatter | solution.py:60
  399.2 1.8 convolution_bitcast_fusion
  401.1 0.0 all-reduce.2.cloned.1.call-update
  401.1 1.8 convolution_convert_fusion.1
  402.9 145.9 %all-reduce.2.cloned.1.call-done = f32[128,256]{0,1:T(8,128)} async-done(((f32[128,256]{0,1:T(8,128)}), f32[128,256]{0,1:T(8,128)}) %all-reduce.2.cloned.1.call-update) | async-done | bytes 131088 | tf_op jit(solution)/shard_map/psum | solution.py:69
  548.8 0.9 broadcast_multiply_fusion.2
  549.7 0.8 copy.12
  (27 shorter events, 0.2 us)
Async XLA Ops:
  7.2 0.8 copy-start
  7.2 40.4 %all-gather.3.cloned.1.call-start = ((), (), s32[]{:S(2)}) async-start(), calls=%async_computation.2 | async-start | bytes 2228224 | tf_op jit(solution)/shard_map/all_gather | solution.py:49
  9.7 186.9 %reduce-scatter.3.cloned.1.call-start = ((), (), s32[]{:S(2)}) async-start(), calls=%async_computation.3 | async-start | bytes 2359296 | tf_op jit(solution)/shard_map/reduce_scatter | solution.py:54
  47.8 148.9 %copy-start.4 = (bf16[256,256]{1,0:T(8,128)(2,1)S(1)}, bf16[256,256]{1,0:T(8,128)(2,1)}, u32[]{:S(2)}) copy-start(bf16[256,256]{1,0:T(8,128)(2,1)} %param.17) | copy-start | bytes 393220
  120.2 1.3 copy-start.1
  121.6 123.7 %all-gather.5.cloned.1.call-start = ((), (), s32[]{:S(2)}) async-start(), calls=%async_computation.4 | async-start | bytes 1179648 | tf_op jit(solution)/shard_map/all_gather | solution.py:57
  198.4 200.8 %reduce-scatter.5.cloned.1.call-start = ((), (), s32[]{:S(2)}) async-start(), calls=%async_computation.5 | async-start | bytes 4456448 | tf_op jit(solution)/shard_map/reduce_scatter | solution.py:60
  245.3 2.4 copy-start.2
  334.9 66.1 %copy-start.3 = (bf16[128,256]{1,0:T(8,128)(2,1)S(1)}, bf16[128,256]{1,0:T(8,128)(2,1)}, u32[]{:S(2)}) copy-start(bf16[128,256]{1,0:T(8,128)(2,1)} %param.12) | copy-start | bytes 196612
  335.0 213.8 %all-reduce.2.cloned.1.call-start = ((), (), s32[]{:S(2)}) async-start(), calls=%async_computation.6 | async-start | bytes 262144 | tf_op jit(solution)/shard_map/psum | solution.py:69
Sparse Core Ops, SparseCore 0:
  10.3 37.2 all-gather.2
  121.7 74.9 reduce-scatter.2
  199.6 45.6 all-gather.4
  335.1 64.0 reduce-scatter.4
  404.4 144.3 all-reduce.1
where the time goes:
time: 558 us; the launch traced here: 557 us
  waiting for transfers between devices  351 us (63%)
  other arithmetic  93.1 us (17%)
  matrix products  52.9 us (9%)
  local copies, waits for them, and re-layouts  45.1 us (8%)
  between operations  14.5 us (3%)
    psum x1, waiting for transfers between devices, body(): grad_weight = lax.psum(local_term, ('row', 'col')) / math.sqrt(nodes)  146 us
    scatter-add x6, other arithmetic, step(): return (total.at[placed].add(product * weights[:, None, None]), None)  90.3 us
    reduce_scatter x1, waiting for transfers between devices, body(): lax.psum_scatter(partial_value, 'col', scatter_dimension=0, tiled=True)  75 us
    reduce_scatter x1, waiting for transfers between devices, body(): lax.psum_scatter(back, 'row', scatter_dimension=0, tiled=True)  64.2 us
    all_gather x1, waiting for transfers between devices, body(): column_rows = lax.all_gather(projected, 'row', axis=0, tiled=True)  35.7 us
    all_gather x1, waiting for transfers between devices, body(): grad_range = lax.all_gather(grad_summed, 'col', axis=0, tiled=True)  30.2 us
    dot_general x3, matrix products, step(): jnp.einsum('sab,sbf->saf', values, picked, preferred_element_type=jnp.flo...  23.8 us
    dot_general x3, matrix products, step(): jnp.einsum('sab,saf->sbf', values, picked, preferred_element_type=jnp.flo...  23.8 us
  transfers between devices with their start and end apart: 5, of which 5 were waited for; matrix products, arithmetic and copies ran while one was open for 4% of the time, Pallas kernels for 0%

commit v1 on v0

--- a/solution.py
+++ b/solution.py
@@ -54,7 +54,9 @@
     summed = lax.psum_scatter(partial_value, "col", scatter_dimension=0, tiled=True)
     output = jax.nn.silu(summed).astype(jnp.bfloat16)
     grad_summed = (cotangent.astype(jnp.float32) * silu_slope(summed)).astype(jnp.bfloat16)
-    grad_range = lax.all_gather(grad_summed, "col", axis=0, tiled=True)
+    grad_range = jnp.concatenate(
+        lax.all_to_all(jnp.stack([grad_summed] * lax.axis_size("col")), "col", 0, 0), axis=0
+    )
     grad_blocks = grad_range.reshape(tile_rows, size, width)
     back = block_product(adj_values, slot_rows, slot_cols, keep, grad_blocks, tile_cols, True)
     grad_projected = lax.psum_scatter(back, "row", scatter_dimension=0, tiled=True).astype(

time: 558 us -> 536 us (0.961)
  waiting for transfers between devices: 351 us -> 324 us
    all_gather x1 -> x0, waiting for transfers between devices: 30.2 us -> none  [body(): grad_range = lax.all_gather(grad_summed, 'col', axis=0, tiled=True)]
    unnamed x12 -> x10, local copies, waits for them, and re-layouts: 19.5 us -> 19.5 us
  transfers between devices with their start and end apart: 5 -> 5, of which waited for: 5 -> 4; matrix products, arithmetic and copies ran while one was open for 4% -> 4% of each run, Pallas kernels for 0% -> 0%
where the time goes in v1:
time: 536 us; the launch traced here: 535 us
  waiting for transfers between devices  324 us (60%)
  other arithmetic  93 us (17%)
  matrix products  52.9 us (10%)
  local copies, waits for them, and re-layouts  46.2 us (9%)
  between operations  14.5 us (3%)
    psum x1, waiting for transfers between devices, body(): grad_weight = lax.psum(local_term, ('row', 'col')) / math.sqrt(nodes)  146 us
    scatter-add x6, other arithmetic, step(): return (total.at[placed].add(product * weights[:, None, None]), None)  90.2 us
    reduce_scatter x1, waiting for transfers between devices, body(): lax.psum_scatter(partial_value, 'col', scatter_dimension=0, tiled=True)  75.1 us
    reduce_scatter x1, waiting for transfers between devices, body(): lax.psum_scatter(back, 'row', scatter_dimension=0, tiled=True)  67.6 us
    all_gather x1, waiting for transfers between devices, body(): column_rows = lax.all_gather(projected, 'row', axis=0, tiled=True)  35.7 us
    dot_general x3, matrix products, step(): jnp.einsum('sab,sbf->saf', values, picked, preferred_element_type=jnp.flo...  23.9 us
    dot_general x3, matrix products, step(): jnp.einsum('sab,saf->sbf', values, picked, preferred_element_type=jnp.flo...  23.8 us
    gather x6, local copies, waits for them, and re-layouts, step(): picked = source[taken]  21.5 us
  transfers between devices with their start and end apart: 5, of which 4 were waited for; matrix products, arithmetic and copies ran while one was open for 4% of the time, Pallas kernels for 0%

profile of v1, /device:TPU:1, one launch (start us, length us, event | category | flops | bytes accessed | tf_op | source)
XLA Modules:
  0.0 534.8 jit_solution(15482427791717770959)
XLA Ops:
  7.2 0.0 copy-start
  7.2 0.0 all-gather.2.cloned.1.call-start
  7.2 0.8 copy-done
  8.0 1.7 convolution_convert_fusion
  9.7 0.0 all-gather.2.cloned.1.call-update
  9.7 0.0 reduce-scatter.3.cloned.1.call-start
  10.4 0.7 reshape.148
  11.1 0.7 reshape.150
  11.9 35.7 %all-gather.2.cloned.1.call-done = bf16[4096,256]{1,0:T(8,128)(2,1)} async-done(((bf16[256,256]{1,0:T(8,128)(2,1)}), bf16[4096,256]{1,0:T(8,128)(2,1)}) %all-gather.2.cloned.1.call-update) | async-done | bytes 2097168 | tf_op jit(solution)/shard_map/all_gather | solution.py:49
  47.6 0.2 broadcast_in_dim.4
  47.8 72.4 %while.20 = (s32[]{:T(128)}, f32[8,256,256]{2,1,0:T(8,128)S(1)}, s32[3,32]{1,0:T(4,128)S(1)}, bf16[3,32,256,256]{3,2,1,0:T(8,128)(2,1)}, s32[3,32]{1,0:T(4,128)S...) while((s32[]{:T(128)}, f32[8,256,256]{2,1,0:T(8,128)S(1)}, s32[3,32]{1,0:T(4,128)S(1)}, ...), condition=%wide.region_2.3_spmd, body=%wide.region_0.2_spmd.sunk | while | flops 1077937408 | bytes 50337628 | solution.py:34
  47.8 4.4 gather_fusion
  52.2 8.0 %broadcast_multiply_fusion.5 = f32[32,256,256]{2,1,0:T(8,128)} fusion(f32[32]{0:T(128)S(1)} %fusion.42, bf16[32,256,256]{2,1,0:T(8,128)(2,1)} %gather_fusion, bf16[3,32,256,256]{3,2,1,0:T(8,128)(2,1)} %get-tuple-element.236, s32[]{:T(128)} %get-tuple-element.225), kind=kOutput, calls=%fused_computation.6.clone.1 | convolution fusion | flops 1075838976 | bytes 16777856 | tf_op jit(solution)/shard_map/while/body/eval_jaxpr/sab,sbf->saf/dot_general | solution.py:25
  60.2 11.8 %scatter_fusion = f32[8,256,256]{2,1,0:T(8,128)S(1)} fusion(f32[8,256,256]{2,1,0:T(8,128)S(1)} %get-tuple-element.226, s32[32]{0:T(128)S(1)} %get-tuple-element.206, f32[32,256,256]{2,1,0:T(8,128)} %broadcast_multiply_fusion.5), kind=kCustom, calls=%fused_computation.2.clone.1 | custom fusion | flops 2097152 | bytes 25165952 | tf_op jit(solution)/shard_map/while/body/eval_jaxpr/scatter-add | solution.py:26
  72.0 4.4 gather_fusion
  76.4 8.0 %broadcast_multiply_fusion.5 = f32[32,256,256]{2,1,0:T(8,128)} fusion(f32[32]{0:T(128)S(1)} %fusion.42, bf16[32,256,256]{2,1,0:T(8,128)(2,1)} %gather_fusion, bf16[3,32,256,256]{3,2,1,0:T(8,128)(2,1)} %get-tuple-element.236, s32[]{:T(128)} %get-tuple-element.225), kind=kOutput, calls=%fused_computation.6.clone.1 | convolution fusion | flops 1075838976 | bytes 16777856 | tf_op jit(solution)/shard_map/while/body/eval_jaxpr/sab,sbf->saf/dot_general | solution.py:25
  84.3 11.7 %scatter_fusion = f32[8,256,256]{2,1,0:T(8,128)S(1)} fusion(f32[8,256,256]{2,1,0:T(8,128)S(1)} %get-tuple-element.226, s32[32]{0:T(128)S(1)} %get-tuple-element.206, f32[32,256,256]{2,1,0:T(8,128)} %broadcast_multiply_fusion.5), kind=kCustom, calls=%fused_computation.2.clone.1 | custom fusion | flops 2097152 | bytes 25165952 | tf_op jit(solution)/shard_map/while/body/eval_jaxpr/scatter-add | solution.py:26
  96.1 4.4 gather_fusion
  100.5 8.0 %broadcast_multiply_fusion.5 = f32[32,256,256]{2,1,0:T(8,128)} fusion(f32[32]{0:T(128)S(1)} %fusion.42, bf16[32,256,256]{2,1,0:T(8,128)(2,1)} %gather_fusion, bf16[3,32,256,256]{3,2,1,0:T(8,128)(2,1)} %get-tuple-element.236, s32[]{:T(128)} %get-tuple-element.225), kind=kOutput, calls=%fused_computation.6.clone.1 | convolution fusion | flops 1075838976 | bytes 16777856 | tf_op jit(solution)/shard_map/while/body/eval_jaxpr/sab,sbf->saf/dot_general | solution.py:25
  108.5 11.7 %scatter_fusion = f32[8,256,256]{2,1,0:T(8,128)S(1)} fusion(f32[8,256,256]{2,1,0:T(8,128)S(1)} %get-tuple-element.226, s32[32]{0:T(128)S(1)} %get-tuple-element.206, f32[32,256,256]{2,1,0:T(8,128)} %broadcast_multiply_fusion.5), kind=kCustom, calls=%fused_computation.2.clone.1 | custom fusion | flops 2097152 | bytes 25165952 | tf_op jit(solution)/shard_map/while/body/eval_jaxpr/scatter-add | solution.py:26
  120.2 1.3 copy-done.1
  121.6 0.0 reduce-scatter.3.cloned.1.call-update
  121.6 75.1 %reduce-scatter.3.cloned.1.call-done = f32[256,256]{1,0:T(8,128)} async-done(((f32[2048,256]{1,0:T(8,128)}), f32[256,256]{1,0:T(8,128)}) %reduce-scatter.3.cloned.1.call-update) | async-done | bytes 262160 | tf_op jit(solution)/shard_map/reduce_scatter | solution.py:54
  196.7 1.7 multiply_convert_fusion
  198.4 1.1 stack.2
  199.5 3.6 all-to-all-start
  203.1 0.0 reduce-scatter.5.cloned.1.call-start
  203.1 16.6 %copy.10 = bf16[96,256,256]{1,2,0:T(8,128)(2,1)} copy(bf16[96,256,256]{2,1,0:T(8,128)(2,1)} %bitcast.85) | data formatting | bytes 25165824 | tf_op args[2]
  219.7 2.4 broadcast_in_dim.8
  222.1 87.2 %while.21 = (s32[]{:T(128)}, f32[16,256,256]{2,1,0:T(8,128)}, s32[3,32]{1,0:T(4,128)S(1)}, bf16[3,32,256,256]{2,3,1,0:T(8,128)(2,1)}, s32[3,32]{1,0:T(4,128)S(1)...) while((s32[]{:T(128)}, f32[16,256,256]{2,1,0:T(8,128)}, s32[3,32]{1,0:T(4,128)S(1)}, ...), condition=%wide.region_6.7_spmd, body=%wide.region_4.6_spmd.sunk | while | flops 1077937408 | bytes 50337628 | solution.py:34
  222.2 2.8 gather_fusion.1
  224.9 7.9 %broadcast_multiply_fusion.6 = f32[32,256,256]{2,1,0:T(8,128)} fusion(f32[32]{0:T(128)S(1)} %fusion.46, bf16[32,256,256]{2,1,0:T(8,128)(2,1)} %gather_fusion.1, bf16[3,32,256,256]{2,3,1,0:T(8,128)(2,1)} %get-tuple-element.260, s32[]{:T(128)} %get-tuple-element.249), kind=kOutput, calls=%fused_computation.22.clone.1 | convolution fusion | flops 1075838976 | bytes 16777856 | tf_op jit(solution)/shard_map/while/body/eval_jaxpr/sab,saf->sbf/dot_general | solution.py:23
  232.9 18.4 %scatter_fusion.1 = f32[16,256,256]{2,1,0:T(8,128)} fusion(f32[16,256,256]{2,1,0:T(8,128)} %get-tuple-element.250, s32[32]{0:T(128)S(1)} %get-tuple-element.215, f32[32,256,256]{2,1,0:T(8,128)} %broadcast_multiply_fusion.6), kind=kCustom, calls=%fused_computation.3.clone.1 | custom fusion | flops 2097152 | bytes 25165952 | tf_op jit(solution)/shard_map/while/body/eval_jaxpr/scatter-add | solution.py:26
  251.3 2.8 gather_fusion.1
  254.1 7.9 %broadcast_multiply_fusion.6 = f32[32,256,256]{2,1,0:T(8,128)} fusion(f32[32]{0:T(128)S(1)} %fusion.46, bf16[32,256,256]{2,1,0:T(8,128)(2,1)} %gather_fusion.1, bf16[3,32,256,256]{2,3,1,0:T(8,128)(2,1)} %get-tuple-element.260, s32[]{:T(128)} %get-tuple-element.249), kind=kOutput, calls=%fused_computation.22.clone.1 | convolution fusion | flops 1075838976 | bytes 16777856 | tf_op jit(solution)/shard_map/while/body/eval_jaxpr/sab,saf->sbf/dot_general | solution.py:23
  262.1 18.3 %scatter_fusion.1 = f32[16,256,256]{2,1,0:T(8,128)} fusion(f32[16,256,256]{2,1,0:T(8,128)} %get-tuple-element.250, s32[32]{0:T(128)S(1)} %get-tuple-element.215, f32[32,256,256]{2,1,0:T(8,128)} %broadcast_multiply_fusion.6), kind=kCustom, calls=%fused_computation.3.clone.1 | custom fusion | flops 2097152 | bytes 25165952 | tf_op jit(solution)/shard_map/while/body/eval_jaxpr/scatter-add | solution.py:26
  280.4 2.8 gather_fusion.1
  283.2 7.9 %broadcast_multiply_fusion.6 = f32[32,256,256]{2,1,0:T(8,128)} fusion(f32[32]{0:T(128)S(1)} %fusion.46, bf16[32,256,256]{2,1,0:T(8,128)(2,1)} %gather_fusion.1, bf16[3,32,256,256]{2,3,1,0:T(8,128)(2,1)} %get-tuple-element.260, s32[]{:T(128)} %get-tuple-element.249), kind=kOutput, calls=%fused_computation.22.clone.1 | convolution fusion | flops 1075838976 | bytes 16777856 | tf_op jit(solution)/shard_map/while/body/eval_jaxpr/sab,saf->sbf/dot_general | solution.py:23
  291.1 18.2 %scatter_fusion.1 = f32[16,256,256]{2,1,0:T(8,128)} fusion(f32[16,256,256]{2,1,0:T(8,128)} %get-tuple-element.250, s32[32]{0:T(128)S(1)} %get-tuple-element.215, f32[32,256,256]{2,1,0:T(8,128)} %broadcast_multiply_fusion.6), kind=kCustom, calls=%fused_computation.3.clone.1 | custom fusion | flops 2097152 | bytes 25165952 | tf_op jit(solution)/shard_map/while/body/eval_jaxpr/scatter-add | solution.py:26
  309.4 0.0 reduce-scatter.5.cloned.1.call-update
  309.4 0.0 all-reduce.2.cloned.1.call-start
  309.4 67.6 %reduce-scatter.5.cloned.1.call-done = f32[256,256]{1,0:T(8,128)} async-done(((f32[4096,256]{1,0:T(8,128)}), f32[256,256]{1,0:T(8,128)}) %reduce-scatter.5.cloned.1.call-update) | async-done | bytes 262160 | tf_op jit(solution)/shard_map/reduce_scatter | solution.py:62
  377.1 1.8 convolution_bitcast_fusion
  378.9 0.0 all-reduce.2.cloned.1.call-update
  378.9 1.8 convolution_convert_fusion.1
  380.7 145.9 %all-reduce.2.cloned.1.call-done = f32[128,256]{0,1:T(8,128)} async-done(((f32[128,256]{0,1:T(8,128)}), f32[128,256]{0,1:T(8,128)}) %all-reduce.2.cloned.1.call-update) | async-done | bytes 131088 | tf_op jit(solution)/shard_map/psum | solution.py:71
  526.6 0.9 broadcast_multiply_fusion.2
  527.5 0.8 copy.12
  (25 shorter events, 0.1 us)
Async XLA Ops:
  7.2 0.8 copy-start
  7.2 40.4 %all-gather.2.cloned.1.call-start = ((), (), s32[]{:S(2)}) async-start(), calls=%async_computation.3 | async-start | bytes 2228224 | tf_op jit(solution)/shard_map/all_gather | solution.py:49
  9.7 187.0 %reduce-scatter.3.cloned.1.call-start = ((), (), s32[]{:S(2)}) async-start(), calls=%async_computation.4 | async-start | bytes 2359296 | tf_op jit(solution)/shard_map/reduce_scatter | solution.py:54
  47.8 148.9 %copy-start.3 = (bf16[256,256]{1,0:T(8,128)(2,1)S(1)}, bf16[256,256]{1,0:T(8,128)(2,1)}, u32[]{:S(2)}) copy-start(bf16[256,256]{1,0:T(8,128)(2,1)} %param.17) | copy-start | bytes 393220
  120.2 1.3 copy-start.1
  199.5 20.2 %all-to-all-start = ((bf16[8,256,256]{2,1,0:T(8,128)(2,1)}), bf16[8,256,256]{2,1,0:T(8,128)(2,1)S(1)}, u32[]{:S(2)}, u32[]{:S(2)}) async-start(bf16[8,256,256]{2,1,0:T(8,128)(2,1)} %stack.2), calls=%async_computation.1 | async-start | bytes 2097152 | tf_op jit(solution)/shard_map/all_to_all | solution.py:58
  203.1 174.0 %reduce-scatter.5.cloned.1.call-start = ((), (), s32[]{:S(2)}) async-start(), calls=%async_computation.5 | async-start | bytes 4456448 | tf_op jit(solution)/shard_map/reduce_scatter | solution.py:62
  309.4 69.6 %copy-start.2 = (bf16[128,256]{1,0:T(8,128)(2,1)S(1)}, bf16[128,256]{1,0:T(8,128)(2,1)}, u32[]{:S(2)}) copy-start(bf16[128,256]{1,0:T(8,128)(2,1)} %param.12) | copy-start | bytes 196612
  309.4 217.2 %all-reduce.2.cloned.1.call-start = ((), (), s32[]{:S(2)}) async-start(), calls=%async_computation.6 | async-start | bytes 262144 | tf_op jit(solution)/shard_map/psum | solution.py:71
Sparse Core Ops, SparseCore 0:
  10.3 37.2 all-gather.1
  121.7 74.9 reduce-scatter.2
  309.5 67.5 reduce-scatter.4
  382.2 144.3 all-reduce.1
